TPU v7x, 256 devices: a whole 4x4x8 slice. The times are simulated.
256 devices in a mesh: leaf: 16 (over x, y), rows: 16 (over z, core).
Axes of the slice: x: 4, y: 4, z: 8, core: 2. Of those that a mesh axis runs over, the one named last changes fastest.
Arguments:
- rhs_top: float32 [1, 4096, 128], P(None, 'rows'), may hold values from -6 to 6
- rhs_one: float32 [2, 2048, 128], P(None, 'rows'), may hold values from -6 to 6
- rhs_two: float32 [4, 2048, 128], P(None, 'rows'), may hold values from -6 to 6
- rhs_three: float32 [8, 1024, 128], P(None, 'rows'), may hold values from -6 to 6
- inv_top: float32 [4096, 4096], P('rows', 'leaf')
- inv_one: float32 [2048, 4096], P('rows', 'leaf')
- inv_two: float32 [2048, 8192], P('rows', 'leaf')
- inv_three: float32 [1024, 8192], P('rows', 'leaf')
- panel_one: float32 [4096, 2048], P('leaf', 'rows'), may hold values from -0.0625 to 0.0625
- panel_two: float32 [8192, 4096], P('leaf', 'rows'), may hold values from -0.0625 to 0.0625
- panel_three: float32 [8192, 4096], P('leaf', 'rows'), may hold values from -0.09375 to 0.09375
- rows_one: int32 [2, 16], P(None, 'rows'), may hold values from 0 to 31, as said below
- rows_two: int32 [4, 32], P(None, 'rows'), may hold values from 0 to 47, as said below
- rows_three: int32 [8, 32], P(None, 'rows'), may hold values from 0 to 63, as said below
Outputs:
- solution_top: float32 [1, 4096, 128], P(None, 'rows')
- solution_one: float32 [2, 2048, 128], P(None, 'rows')
- solution_two: float32 [4, 2048, 128], P(None, 'rows')
- solution_three: float32 [8, 1024, 128], P(None, 'rows')
Inputs may be any that keep to these rules, and one draw needn't show every extreme that they name: `rows_one`: each row lists 16 different blocks of a chain of 32 blocks, the chain's first and last among them. `rows_two`: each row lists 32 different blocks of a chain of 48 blocks, the chain's first and last among them. `rows_three`: each row lists 32 different blocks of a chain of 64 blocks, the chain's first and last among them.
All inputs are finite; a program needn't handle non-finite values.
Results may differ from a plain program's by a relative error of at most 0.0001.
Values sent between devices are 32-bit elements; how exact they have to be, the bound alone decides.
A program may use at most 64 MiB of HBM per device.

v0:
```python
import jax
import jax.numpy as jnp
from jax import lax
from jax.sharding import PartitionSpec as P

SEP0 = 4096
SEP1 = 2048
SEP2 = 2048
SEP3 = 1024
BLOCK = 128


def layout(sep_count, sep_size):
    span_rows = sep_count * sep_size // lax.axis_size("leaf")
    held_count = max(1, span_rows // sep_size)
    part_rows = min(span_rows, sep_size)
    first_sep = lax.axis_index("leaf") * span_rows // sep_size
    return (held_count, part_rows, first_sep)


def forward_solve(inverse, source, sep_count, sep_size):
    held_count, part_rows, first_sep = layout(sep_count, sep_size)
    picked = lax.dynamic_slice_in_dim(source, first_sep, held_count, 0)
    blocks = inverse.reshape(inverse.shape[0], held_count, part_rows)
    partial_y = jnp.einsum("csr,scn->srn", blocks, picked, precision=lax.Precision.HIGHEST)
    return lax.psum(partial_y, "rows")


def chain_matches(index_rows, first_sep, held_count, chain_count, listed):
    picked_rows = lax.dynamic_slice_in_dim(index_rows, first_sep, held_count, 0)
    column_ids = lax.broadcasted_iota(jnp.int32, (held_count, chain_count, listed), 1)
    return (column_ids == picked_rows[:, None, :]).astype(jnp.float32)


def ancestor_terms(panel, index_rows, solved_rows, sep_sizes, sep_counts, level_at):
    held_count, part_rows, first_sep = layout(sep_counts[level_at], sep_sizes[level_at])
    width_rhs = solved_rows.shape[2]
    listed = panel.shape[1] // BLOCK
    chain_count = sum(sep_sizes[:level_at]) // BLOCK
    panel_cut = panel.reshape(held_count, part_rows, listed * BLOCK)
    updates = jnp.einsum("sra,srn->san", panel_cut, solved_rows, precision=lax.Precision.HIGHEST)
    matches = chain_matches(index_rows, first_sep, held_count, chain_count, listed)
    spread = jnp.einsum(
        "sck,skbn->scbn",
        matches,
        updates.reshape(held_count, listed, BLOCK, width_rhs),
        precision=lax.Precision.HIGHEST,
    )
    owners = first_sep + jnp.arange(held_count, dtype=jnp.int32)
    results = []
    offset = 0
    for upper in range(level_at):
        blocks_up = sep_sizes[upper] // BLOCK
        segment = spread[:, offset : offset + blocks_up].reshape(
            held_count, sep_sizes[upper], width_rhs
        )
        target_ids = lax.broadcasted_iota(jnp.int32, (held_count, sep_counts[upper]), 1)
        target = (target_ids == (owners >> level_at - upper)[:, None]).astype(jnp.float32)
        results.append(jnp.einsum("sq,srn->qrn", target, segment, precision=lax.Precision.HIGHEST))
        offset = offset + blocks_up
    return results


def reduce_dense(parts):
    column_parts = lax.psum_scatter(parts, "rows", scatter_dimension=1, tiled=True)
    return lax.psum(column_parts, "leaf")


def backward_panel(panel, index_rows, gathered, solved_rows, sep_sizes, sep_counts, level_at):
    held_count, part_rows, first_sep = layout(sep_counts[level_at], sep_sizes[level_at])
    width_rhs = solved_rows.shape[2]
    listed = panel.shape[1] // BLOCK
    chain_count = sum(sep_sizes[:level_at]) // BLOCK
    owners = first_sep + jnp.arange(held_count, dtype=jnp.int32)
    pieces = []
    for upper in range(level_at):
        target_ids = lax.broadcasted_iota(jnp.int32, (held_count, sep_counts[upper]), 1)
        target = (target_ids == (owners >> level_at - upper)[:, None]).astype(jnp.float32)
        pieces.append(
            jnp.einsum("sq,qrn->srn", target, gathered[upper], precision=lax.Precision.HIGHEST)
        )
    chain_x = jnp.concatenate(pieces, axis=1).reshape(held_count, chain_count, BLOCK, width_rhs)
    matches = chain_matches(index_rows, first_sep, held_count, chain_count, listed)
    chosen = jnp.einsum("sck,scbn->skbn", matches, chain_x, precision=lax.Precision.HIGHEST)
    panel_cut = panel.reshape(held_count, part_rows, listed * BLOCK)
    partial_g = jnp.einsum(
        "sra,san->srn",
        panel_cut,
        chosen.reshape(held_count, listed * BLOCK, width_rhs),
        precision=lax.Precision.HIGHEST,
    )
    return solved_rows - lax.psum(partial_g, "rows")


def backward_solve(inverse, residue, sep_count, sep_size):
    held_count, part_rows, first_sep = layout(sep_count, sep_size)
    blocks = inverse.reshape(inverse.shape[0], held_count, part_rows)
    partial_x = jnp.einsum("csr,srn->scn", blocks, residue, precision=lax.Precision.HIGHEST)
    owners = first_sep + jnp.arange(held_count, dtype=jnp.int32)
    place_ids = lax.broadcasted_iota(jnp.int32, (held_count, sep_count), 1)
    placing = (place_ids == owners[:, None]).astype(jnp.float32)
    dense = jnp.einsum("sq,scn->qcn", placing, partial_x, precision=lax.Precision.HIGHEST)
    return lax.psum(dense, "leaf")


def body(
    rhs_top,
    rhs_one,
    rhs_two,
    rhs_three,
    inv_top,
    inv_one,
    inv_two,
    inv_three,
    panel_one,
    panel_two,
    panel_three,
    rows_one,
    rows_two,
    rows_three,
):
    sep_sizes = [SEP0, SEP1, SEP2, SEP3]
    sep_counts = [1, 2, 4, 8]
    right_sides = [rhs_top, rhs_one, rhs_two, rhs_three]
    inverses = [inv_top, inv_one, inv_two, inv_three]
    panels = [None, panel_one, panel_two, panel_three]
    indices = [None, rows_one, rows_two, rows_three]
    solved = [None, None, None, None]
    owed_rows = [jnp.zeros(item.shape, jnp.float32) for item in right_sides]
    for level_at in (3, 2, 1, 0):
        source = right_sides[level_at] - owed_rows[level_at]
        solved[level_at] = forward_solve(
            inverses[level_at], source, sep_counts[level_at], sep_sizes[level_at]
        )
        if level_at > 0:
            fresh = ancestor_terms(
                panels[level_at],
                indices[level_at],
                solved[level_at],
                sep_sizes,
                sep_counts,
                level_at,
            )
            reduced = reduce_dense(tuple(fresh))
            for upper in range(level_at):
                owed_rows[upper] = owed_rows[upper] + reduced[upper]
    gathered = []
    results = []
    for level_at in range(4):
        residue = solved[level_at]
        if level_at > 0:
            residue = backward_panel(
                panels[level_at],
                indices[level_at],
                gathered,
                solved[level_at],
                sep_sizes,
                sep_counts,
                level_at,
            )
        solution_cols = backward_solve(
            inverses[level_at], residue, sep_counts[level_at], sep_sizes[level_at]
        )
        results.append(solution_cols)
        if level_at < 3:
            gathered.append(lax.all_gather(solution_cols, "rows", axis=1, tiled=True))
    return (results[0], results[1], results[2], results[3])


def solution(mesh):
    return jax.shard_map(
        body,
        mesh=mesh,
        in_specs=(
            P(None, "rows", None),
            P(None, "rows", None),
            P(None, "rows", None),
            P(None, "rows", None),
            P("rows", "leaf"),
            P("rows", "leaf"),
            P("rows", "leaf"),
            P("rows", "leaf"),
            P("leaf", "rows"),
            P("leaf", "rows"),
            P("leaf", "rows"),
            P(None, "rows"),
            P(None, "rows"),
            P(None, "rows"),
        ),
        out_specs=(
            P(None, "rows", None),
            P(None, "rows", None),
            P(None, "rows", None),
            P(None, "rows", None),
        ),
        check_vma=False,
    )
```

profile of v0, /device:TPU:2, one launch (start us, length us, event | category | flops | bytes accessed | tf_op | source)
XLA Modules:
  0.0 1859.5 jit_solution(8080732922114036708)
XLA Ops:
  10.3 113.3 %all-reduce.15.cloned.1.call-done = f32[1,512,128]{1,2,0:T(8,128)} async-done(((f32[1,512,128]{1,2,0:T(8,128)}), f32[1,512,128]{1,2,0:T(8,128)}) %all-reduce.15.cloned.1.call-update) | async-done | bytes 262160 | tf_op jit(solution)/shard_map/psum | solution.py:26
  132.0 63.9 %reduce-scatter.4.cloned.1.call-done = f32[4,128,128]{2,1,0:T(8,128)} async-done(((f32[4,2048,128]{2,1,0:T(8,128)}), f32[4,128,128]{2,1,0:T(8,128)}) %reduce-scatter.4.cloned.1.call-update) | async-done | bytes 262160 | tf_op jit(solution)/shard_map/reduce_scatter | solution.py:65
  196.0 96.3 %all-reduce.17.cloned.1.call-done = f32[4,128,128]{2,1,0:T(8,128)} async-done(((f32[4,128,128]{2,1,0:T(8,128)}), f32[4,128,128]{2,1,0:T(8,128)}) %all-reduce.17.cloned.1.call-update) | async-done | bytes 262160 | tf_op jit(solution)/shard_map/psum | solution.py:66
  294.9 109.9 %all-reduce.19.cloned.1.call-done = f32[1,512,128]{1,2,0:T(8,128)} async-done(((f32[1,512,128]{1,2,0:T(8,128)}), f32[1,512,128]{1,2,0:T(8,128)}) %all-reduce.19.cloned.1.call-update) | async-done | bytes 262160 | tf_op jit(solution)/shard_map/psum | solution.py:26
  411.4 60.6 %reduce-scatter.6.cloned.1.call-done = f32[2,128,128]{2,1,0:T(8,128)} async-done(((f32[2,2048,128]{2,1,0:T(8,128)}), f32[2,128,128]{2,1,0:T(8,128)}) %reduce-scatter.6.cloned.1.call-update) | async-done | bytes 131088 | tf_op jit(solution)/shard_map/reduce_scatter | solution.py:65
  473.3 93.1 %all-reduce.39.cloned.1.call-done = f32[2,128,128]{2,1,0:T(8,128)} async-done(((f32[2,128,128]{2,1,0:T(8,128)}), f32[2,128,128]{2,1,0:T(8,128)}) %all-reduce.39.cloned.1.call-update) | async-done | bytes 131088 | tf_op jit(solution)/shard_map/psum | solution.py:66
  568.3 2.8 fusion.2
  572.3 106.2 %all-reduce.21.cloned.1.call-done = f32[1,256,128]{1,2,0:T(8,128)} async-done(((f32[1,256,128]{1,2,0:T(8,128)}), f32[1,256,128]{1,2,0:T(8,128)}) %all-reduce.21.cloned.1.call-update) | async-done | bytes 131088 | tf_op jit(solution)/shard_map/psum | solution.py:26
  681.7 60.9 %reduce-scatter.8.cloned.1.call-done = f32[1,256,128]{2,1,0:T(8,128)} async-done(((f32[1,4096,128]{2,1,0:T(8,128)}), f32[1,256,128]{2,1,0:T(8,128)}) %reduce-scatter.8.cloned.1.call-update) | async-done | bytes 131088 | tf_op jit(solution)/shard_map/reduce_scatter | solution.py:65
  742.6 94.3 %all-reduce.41.cloned.1.call-done = f32[1,256,128]{2,1,0:T(8,128)} async-done(((f32[1,256,128]{2,1,0:T(8,128)}), f32[1,256,128]{2,1,0:T(8,128)}) %all-reduce.41.cloned.1.call-update) | async-done | bytes 131088 | tf_op jit(solution)/shard_map/psum | solution.py:66
  839.0 109.9 %all-reduce.23.cloned.1.call-done = f32[256,128]{0,1:T(8,128)} async-done(((f32[256,128]{0,1:T(8,128)}), f32[256,128]{0,1:T(8,128)}) %all-reduce.23.cloned.1.call-update) | async-done | bytes 131088 | tf_op jit(solution)/shard_map/psum | solution.py:26
  951.0 95.2 %all-reduce.25.cloned.1.call-done = f32[1,256,128]{1,2,0:T(8,128)} async-done(((f32[1,256,128]{1,2,0:T(8,128)}), f32[1,256,128]{1,2,0:T(8,128)}) %all-reduce.25.cloned.1.call-update) | async-done | bytes 131088 | tf_op jit(solution)/shard_map/psum | solution.py:103
  1046.4 40.7 %all-gather.4.cloned.1.call-done = f32[1,4096,128]{1,2,0:T(8,128)} async-done(((f32[1,256,128]{1,2,0:T(8,128)}), f32[1,4096,128]{1,2,0:T(8,128)}) %all-gather.4.cloned.1.call-update) | async-done | bytes 2097168 | tf_op jit(solution)/shard_map/all_gather | solution.py:166
  1087.2 3.7 broadcast_multiply_fusion.1
  1093.8 107.9 %all-reduce.27.cloned.1.call-done = f32[1,256,128]{1,2,0:T(8,128)} async-done(((f32[1,256,128]{1,2,0:T(8,128)}), f32[1,256,128]{1,2,0:T(8,128)}) %all-reduce.27.cloned.1.call-update) | async-done | bytes 131088 | tf_op jit(solution)/shard_map/psum | solution.py:92
  1203.7 95.0 %all-reduce.29.cloned.1.call-done = f32[2,128,128]{2,1,0:T(8,128)} async-done(((f32[2,128,128]{2,1,0:T(8,128)}), f32[2,128,128]{2,1,0:T(8,128)}) %all-reduce.29.cloned.1.call-update) | async-done | bytes 131088 | tf_op jit(solution)/shard_map/psum | solution.py:103
  1298.8 40.9 %all-gather.6.cloned.1.call-done = f32[2,2048,128]{2,1,0:T(8,128)} async-done(((f32[2,128,128]{2,1,0:T(8,128)}), f32[2,2048,128]{2,1,0:T(8,128)}) %all-gather.6.cloned.1.call-update) | async-done | bytes 2097168 | tf_op jit(solution)/shard_map/all_gather | solution.py:166
  1339.7 7.6 fusion.5
  1347.3 3.6 copy.42
  1354.5 3.6 copy.34
  1358.1 3.0 fusion.33
  1362.7 108.2 %all-reduce.31.cloned.1.call-done = f32[1,512,128]{1,2,0:T(8,128)} async-done(((f32[1,512,128]{1,2,0:T(8,128)}), f32[1,512,128]{1,2,0:T(8,128)}) %all-reduce.31.cloned.1.call-update) | async-done | bytes 262160 | tf_op jit(solution)/shard_map/psum | solution.py:92
  1473.2 96.5 %all-reduce.33.cloned.1.call-done = f32[4,128,128]{2,1,0:T(8,128)} async-done(((f32[4,128,128]{2,1,0:T(8,128)}), f32[4,128,128]{2,1,0:T(8,128)}) %all-reduce.33.cloned.1.call-update) | async-done | bytes 262160 | tf_op jit(solution)/shard_map/psum | solution.py:103
  1570.0 6.6 fusion.3
  1578.5 34.7 %all-gather.8.cloned.1.call-done = f32[4,2048,128]{2,1,0:T(8,128)} async-done(((f32[4,128,128]{2,1,0:T(8,128)}), f32[4,2048,128]{2,1,0:T(8,128)}) %all-gather.8.cloned.1.call-update) | async-done | bytes 4194320 | tf_op jit(solution)/shard_map/all_gather | solution.py:166
  1613.1 9.6 fusion
  1622.7 3.8 copy.45
  1628.4 2.7 copy.48
  1631.1 5.5 copy.37
  1636.6 3.7 fusion.36
  1641.9 108.6 %all-reduce.35.cloned.1.call-done = f32[1,512,128]{1,2,0:T(8,128)} async-done(((f32[1,512,128]{1,2,0:T(8,128)}), f32[1,512,128]{1,2,0:T(8,128)}) %all-reduce.35.cloned.1.call-update) | async-done | bytes 262160 | tf_op jit(solution)/shard_map/psum | solution.py:92
  1753.4 95.9 %all-reduce.37.cloned.1.call-done = f32[8,64,128]{2,1,0:T(8,128)} async-done(((f32[8,64,128]{2,1,0:T(8,128)}), f32[8,64,128]{2,1,0:T(8,128)}) %all-reduce.37.cloned.1.call-update) | async-done | bytes 262160 | tf_op jit(solution)/shard_map/psum | solution.py:103
  (138 shorter events, 56.3 us)
Async XLA Ops:
  7.2 397.6 %copy-start = (f32[512,256]{1,0:T(8,128)S(1)}, f32[512,256]{1,0:T(8,128)}, u32[]{:S(2)}) copy-start(f32[512,256]{1,0:T(8,128)} %param.23) | copy-start | bytes 1572868
  7.2 116.4 %all-reduce.15.cloned.1.call-start = ((), (), s32[]{:S(2)}) async-start(), calls=%async_computation.3 | async-start | bytes 524288 | tf_op jit(solution)/shard_map/psum | solution.py:26
  9.4 186.5 %reduce-scatter.4.cloned.1.call-start = ((), (), s32[]{:S(2)}) async-start(), calls=%async_computation.4 | async-start | bytes 4456448 | tf_op jit(solution)/shard_map/reduce_scatter | solution.py:65
  131.9 160.4 %copy-start.8 = (f32[128,512]{1,0:T(8,128)S(1)}, f32[128,512]{1,0:T(8,128)}, u32[]{:S(2)}) copy-start(f32[128,512]{1,0:T(8,128)} %param.20) | copy-start | bytes 786436
  131.9 162.4 %copy-start.18 = (s32[4,2]{0,1:T(2,128)S(1)}, s32[4,2]{0,1:T(2,128)}, u32[]{:S(2)}) copy-start(s32[4,2]{0,1:T(2,128)} %param.26) | copy-start | bytes 100
  132.0 160.3 %all-reduce.17.cloned.1.call-start = ((), (), s32[]{:S(2)}) async-start(), calls=%async_computation.5 | async-start | bytes 524288 | tf_op jit(solution)/shard_map/psum | solution.py:66
  195.9 208.9 %all-reduce.19.cloned.1.call-start = ((), (), s32[]{:S(2)}) async-start(), calls=%async_computation.6 | async-start | bytes 524288 | tf_op jit(solution)/shard_map/psum | solution.py:26
  294.3 177.6 %reduce-scatter.6.cloned.1.call-start = ((), (), s32[]{:S(2)}) async-start(), calls=%async_computation.21 | async-start | bytes 2228224 | tf_op jit(solution)/shard_map/reduce_scatter | solution.py:65
  411.3 155.1 %copy-start.10 = (f32[128,256]{1,0:T(8,128)S(1)}, f32[128,256]{1,0:T(8,128)}, u32[]{:S(2)}) copy-start(f32[128,256]{1,0:T(8,128)} %param.19) | copy-start | bytes 393220
  411.3 155.1 %copy-start.17 = (f32[2,128,128]{2,1,0:T(8,128)S(1)}, f32[2,128,128]{2,1,0:T(8,128)}, u32[]{:S(2)}) copy-start(f32[2,128,128]{2,1,0:T(8,128)} %param.15) | copy-start | bytes 393220
  411.3 155.1 %all-reduce.39.cloned.1.call-start = ((), (), s32[]{:S(2)}) async-start(), calls=%async_computation.19 | async-start | bytes 262144 | tf_op jit(solution)/shard_map/psum | solution.py:66
  472.0 206.5 %all-reduce.21.cloned.1.call-start = ((), (), s32[]{:S(2)}) async-start(), calls=%async_computation.7 | async-start | bytes 262144 | tf_op jit(solution)/shard_map/psum | solution.py:26
  568.2 174.4 %reduce-scatter.8.cloned.1.call-start = ((), (), s32[]{:S(2)}) async-start(), calls=%async_computation.22 | async-start | bytes 2228224 | tf_op jit(solution)/shard_map/reduce_scatter | solution.py:65
  681.6 155.3 %copy-start.7 = (f32[256,256]{1,0:T(8,128)S(1)}, f32[256,256]{1,0:T(8,128)}, u32[]{:S(2)}) copy-start(f32[256,256]{1,0:T(8,128)} %param.18) | copy-start | bytes 786436
  681.6 155.3 %copy-start.16 = (f32[1,256,128]{2,1,0:T(8,128)S(1)}, f32[1,256,128]{2,1,0:T(8,128)}, u32[]{:S(2)}) copy-start(f32[1,256,128]{2,1,0:T(8,128)} %param.14) | copy-start | bytes 393220
  681.7 155.3 %all-reduce.41.cloned.1.call-start = ((), (), s32[]{:S(2)}) async-start(), calls=%async_computation.20 | async-start | bytes 262144 | tf_op jit(solution)/shard_map/psum | solution.py:66
  742.6 206.3 %all-reduce.23.cloned.1.call-start = ((), (), s32[]{:S(2)}) async-start(), calls=%async_computation.8 | async-start | bytes 262144 | tf_op jit(solution)/shard_map/psum | solution.py:26
  838.9 207.2 %all-reduce.25.cloned.1.call-start = ((), (), s32[]{:S(2)}) async-start(), calls=%async_computation.9 | async-start | bytes 262144 | tf_op jit(solution)/shard_map/psum | solution.py:103
  950.9 136.2 %all-gather.4.cloned.1.call-start = ((), (), s32[]{:S(2)}) async-start(), calls=%async_computation.10 | async-start | bytes 2228224 | tf_op jit(solution)/shard_map/all_gather | solution.py:166
  1046.2 155.4 %all-reduce.27.cloned.1.call-start = ((), (), s32[]{:S(2)}) async-start(), calls=%async_computation.11 | async-start | bytes 262144 | tf_op jit(solution)/shard_map/psum | solution.py:92
  1093.7 205.0 %all-reduce.29.cloned.1.call-start = ((), (), s32[]{:S(2)}) async-start(), calls=%async_computation.12 | async-start | bytes 262144 | tf_op jit(solution)/shard_map/psum | solution.py:103
  1203.7 136.0 %all-gather.6.cloned.1.call-start = ((), (), s32[]{:S(2)}) async-start(), calls=%async_computation.13 | async-start | bytes 2228224 | tf_op jit(solution)/shard_map/all_gather | solution.py:166
  1298.7 172.2 %all-reduce.31.cloned.1.call-start = ((), (), s32[]{:S(2)}) async-start(), calls=%async_computation.14 | async-start | bytes 524288 | tf_op jit(solution)/shard_map/psum | solution.py:92
  1358.1 112.8 %copy-start.6 = (f32[1,512,128]{1,2,0:T(8,128)S(1)}, f32[1,512,128]{1,2,0:T(8,128)}, u32[]{:S(2)}) copy-start(f32[1,512,128]{1,2,0:T(8,128)} %all-reduce.19.cloned.1.call-done) | copy-start | bytes 786436
  1362.6 207.1 %all-reduce.33.cloned.1.call-start = ((), (), s32[]{:S(2)}) async-start(), calls=%async_computation.15 | async-start | bytes 524288 | tf_op jit(solution)/shard_map/psum | solution.py:103
  1473.2 140.0 %all-gather.8.cloned.1.call-start = ((), (), s32[]{:S(2)}) async-start(), calls=%async_computation.16 | async-start | bytes 4456448 | tf_op jit(solution)/shard_map/all_gather | solution.py:166
  1569.7 180.7 %all-reduce.35.cloned.1.call-start = ((), (), s32[]{:S(2)}) async-start(), calls=%async_computation.17 | async-start | bytes 524288 | tf_op jit(solution)/shard_map/psum | solution.py:92
  1636.6 113.9 %copy-start.5 = (f32[1,512,128]{1,2,0:T(8,128)S(1)}, f32[1,512,128]{1,2,0:T(8,128)}, u32[]{:S(2)}) copy-start(f32[1,512,128]{1,2,0:T(8,128)} %all-reduce.15.cloned.1.call-done) | copy-start | bytes 786436
  1636.6 113.9 %copy-start.15 = (f32[64,512]{1,0:T(8,128)S(1)}, f32[64,512]{1,0:T(8,128)}, u32[]{:S(2)}) copy-start(f32[64,512]{1,0:T(8,128)} %param.21) | copy-start | bytes 393220
  1640.3 209.0 %copy-start.14 = (f32[2,128,128]{2,1,0:T(8,128)S(1)}, f32[2,128,128]{2,1,0:T(8,128)}, u32[]{:S(2)}) copy-start(f32[2,128,128]{2,1,0:T(8,128)} %all-reduce.29.cloned.1.call-done) | copy-start | bytes 393220
  1640.3 209.6 %copy-start.9 = (f32[4,128,128]{2,1,0:T(8,128)S(1)}, f32[4,128,128]{2,1,0:T(8,128)}, u32[]{:S(2)}) copy-start(f32[4,128,128]{2,1,0:T(8,128)} %all-reduce.33.cloned.1.call-done) | copy-start | bytes 786436
  1641.8 207.5 %all-reduce.37.cloned.1.call-start = ((), (), s32[]{:S(2)}) async-start(), calls=%async_computation.18 | async-start | bytes 524288 | tf_op jit(solution)/shard_map/psum | solution.py:103
  (8 other events, 402.2 us)
Sparse Core Ops, SparseCore 0:
  10.9 112.7 all-reduce.14
  132.1 63.7 reduce-scatter.3
  199.0 93.1 all-reduce.16
  295.0 109.7 all-reduce.18
  411.4 60.4 reduce-scatter.5
  475.0 91.3 all-reduce.38
  569.3 109.2 all-reduce.20
  681.8 60.7 reduce-scatter.7
  745.8 91.1 all-reduce.40
  839.7 109.1 all-reduce.22
  952.7 93.4 all-reduce.24
  1047.9 39.2 all-gather.3
  1093.8 107.7 all-reduce.26
  1205.2 93.4 all-reduce.28
  1300.4 39.2 all-gather.5
  1362.7 108.1 all-reduce.30
  1474.5 95.1 all-reduce.32
  1571.4 41.6 all-gather.7
  1641.9 108.4 all-reduce.34
  1754.1 95.1 all-reduce.36
where the time goes:
time: 1870 us; the launch traced here: 1860 us
  waiting for transfers between devices  1730 us (93%)
  matrix products  56.9 us (3%)
  local copies, waits for them, and re-layouts  35.2 us (2%)
  other arithmetic  18.7 us (1%)
    psum x4, waiting for transfers between devices, forward_solve(): return lax.psum(partial_y, 'rows')  439 us
    psum x4, waiting for transfers between devices, backward_solve(): return lax.psum(dense, 'leaf')  383 us
    psum x3, waiting for transfers between devices, backward_panel(): return solved_rows - lax.psum(partial_g, 'rows')  325 us
    psum x3, waiting for transfers between devices, reduce_dense(): return lax.psum(column_parts, 'leaf')  284 us
    reduce_scatter x3, waiting for transfers between devices, reduce_dense(): lax.psum_scatter(parts, 'rows', scatter_dimension=1, tiled=True)  185 us
    all_gather x3, waiting for transfers between devices, body(): gathered.append(lax.all_gather(solution_cols, 'rows', axis=1, tiled=True))  116 us
  transfers between devices with their start and end apart: 20, of which 20 were waited for; matrix products, arithmetic and copies ran while one was open for 1% of the time, Pallas kernels for 0%

commit v1 on v0

--- a/solution.py
+++ b/solution.py
@@ -8,6 +8,12 @@
 SEP2 = 2048
 SEP3 = 1024
 BLOCK = 128
+
+
+def summed_here(block, axis):
+    parts = lax.all_gather(block, axis, axis=0, tiled=False)
+    summed = parts.sum(axis=0)
+    return summed
 
 
 def layout(sep_count, sep_size):
@@ -23,7 +29,7 @@
     picked = lax.dynamic_slice_in_dim(source, first_sep, held_count, 0)
     blocks = inverse.reshape(inverse.shape[0], held_count, part_rows)
     partial_y = jnp.einsum("csr,scn->srn", blocks, picked, precision=lax.Precision.HIGHEST)
-    return lax.psum(partial_y, "rows")
+    return summed_here(partial_y, "rows")
 
 
 def chain_matches(index_rows, first_sep, held_count, chain_count, listed):

time: 1870 us -> 1600 us (0.86)
  waiting for transfers between devices: 1730 us -> 1440 us
    psum x4 -> x0, waiting for transfers between devices: 439 us -> none  [forward_solve(): return lax.psum(partial_y, 'rows')]
    all_gather x0 -> x4, waiting for transfers between devices: none -> 160 us  [summed_here(): parts = lax.all_gather(block, axis, axis=0, tiled=False)]
where the time goes in v1:
time: 1600 us; the launch traced here: 1590 us
  waiting for transfers between devices  1440 us (90%)
  matrix products  54.2 us (3%)
  local copies, waits for them, and re-layouts  53.7 us (3%)
  other arithmetic  22 us (1%)
    psum x4, waiting for transfers between devices, backward_solve(): return lax.psum(dense, 'leaf')  377 us
    psum x3, waiting for transfers between devices, backward_panel(): return solved_rows - lax.psum(partial_g, 'rows')  325 us
    psum x3, waiting for transfers between devices, reduce_dense(): return lax.psum(column_parts, 'leaf')  285 us
    reduce_scatter x3, waiting for transfers between devices, reduce_dense(): lax.psum_scatter(parts, 'rows', scatter_dimension=1, tiled=True)  179 us
    all_gather x4, waiting for transfers between devices, summed_here(): parts = lax.all_gather(block, axis, axis=0, tiled=False)  160 us
    all_gather x3, waiting for transfers between devices, body(): gathered.append(lax.all_gather(solution_cols, 'rows', axis=1, tiled=True))  117 us
  transfers between devices with their start and end apart: 20, of which 20 were waited for; matrix products, arithmetic and copies ran while one was open for 1% of the time, Pallas kernels for 0%

profile of v1, /device:TPU:2, one launch (start us, length us, event | category | flops | bytes accessed | tf_op | source)
XLA Modules:
  0.0 1589.5 jit_solution(6960801663441611233)
XLA Ops:
  10.3 45.0 %all-gather.18.cloned.1.call-done = f32[8192,128]{0,1:T(8,128)} async-done(((f32[512,128]{0,1:T(8,128)}), f32[8192,128]{0,1:T(8,128)}) %all-gather.18.cloned.1.call-update) | async-done | bytes 4194320 | tf_op jit(solution)/shard_map/all_gather | solution.py:14
  55.3 5.4 copy.60
  69.0 62.1 %reduce-scatter.4.cloned.1.call-done = f32[4,128,128]{2,1,0:T(8,128)} async-done(((f32[4,2048,128]{2,1,0:T(8,128)}), f32[4,128,128]{2,1,0:T(8,128)}) %reduce-scatter.4.cloned.1.call-update) | async-done | bytes 262160 | tf_op jit(solution)/shard_map/reduce_scatter | solution.py:71
  131.2 96.1 %all-reduce.11.cloned.1.call-done = f32[4,128,128]{2,1,0:T(8,128)} async-done(((f32[4,128,128]{2,1,0:T(8,128)}), f32[4,128,128]{2,1,0:T(8,128)}) %all-reduce.11.cloned.1.call-update) | async-done | bytes 262160 | tf_op jit(solution)/shard_map/psum | solution.py:72
  230.2 41.2 %all-gather.20.cloned.1.call-done = f32[8192,128]{0,1:T(8,128)} async-done(((f32[512,128]{0,1:T(8,128)}), f32[8192,128]{0,1:T(8,128)}) %all-gather.20.cloned.1.call-update) | async-done | bytes 4194320 | tf_op jit(solution)/shard_map/all_gather | solution.py:14
  271.4 5.4 copy.61
  283.3 58.6 %reduce-scatter.6.cloned.1.call-done = f32[2,128,128]{2,1,0:T(8,128)} async-done(((f32[2,2048,128]{2,1,0:T(8,128)}), f32[2,128,128]{2,1,0:T(8,128)}) %reduce-scatter.6.cloned.1.call-update) | async-done | bytes 131088 | tf_op jit(solution)/shard_map/reduce_scatter | solution.py:71
  342.1 94.3 %all-reduce.27.cloned.1.call-done = f32[2,128,128]{2,1,0:T(8,128)} async-done(((f32[2,128,128]{2,1,0:T(8,128)}), f32[2,128,128]{2,1,0:T(8,128)}) %all-reduce.27.cloned.1.call-update) | async-done | bytes 131088 | tf_op jit(solution)/shard_map/psum | solution.py:72
  443.5 34.6 %all-gather.22.cloned.1.call-done = f32[4096,128]{0,1:T(8,128)} async-done(((f32[256,128]{0,1:T(8,128)}), f32[4096,128]{0,1:T(8,128)}) %all-gather.22.cloned.1.call-update) | async-done | bytes 2097168 | tf_op jit(solution)/shard_map/all_gather | solution.py:14
  486.5 58.4 %reduce-scatter.8.cloned.1.call-done = f32[1,256,128]{2,1,0:T(8,128)} async-done(((f32[1,4096,128]{2,1,0:T(8,128)}), f32[1,256,128]{2,1,0:T(8,128)}) %reduce-scatter.8.cloned.1.call-update) | async-done | bytes 131088 | tf_op jit(solution)/shard_map/reduce_scatter | solution.py:71
  545.4 94.3 %all-reduce.29.cloned.1.call-done = f32[1,256,128]{2,1,0:T(8,128)} async-done(((f32[1,256,128]{2,1,0:T(8,128)}), f32[1,256,128]{2,1,0:T(8,128)}) %all-reduce.29.cloned.1.call-update) | async-done | bytes 131088 | tf_op jit(solution)/shard_map/psum | solution.py:72
  641.7 39.5 %all-gather.24.cloned.1.call-done = f32[4096,128]{0,1:T(8,128)} async-done(((f32[256,128]{0,1:T(8,128)}), f32[4096,128]{0,1:T(8,128)}) %all-gather.24.cloned.1.call-update) | async-done | bytes 2097168 | tf_op jit(solution)/shard_map/all_gather | solution.py:14
  685.0 91.3 %all-reduce.13.cloned.1.call-done = f32[1,256,128]{1,2,0:T(8,128)} async-done(((f32[1,256,128]{1,2,0:T(8,128)}), f32[1,256,128]{1,2,0:T(8,128)}) %all-reduce.13.cloned.1.call-update) | async-done | bytes 131088 | tf_op jit(solution)/shard_map/psum | solution.py:109
  776.4 40.9 %all-gather.12.cloned.1.call-done = f32[1,4096,128]{1,2,0:T(8,128)} async-done(((f32[1,256,128]{1,2,0:T(8,128)}), f32[1,4096,128]{1,2,0:T(8,128)}) %all-gather.12.cloned.1.call-update) | async-done | bytes 2097168 | tf_op jit(solution)/shard_map/all_gather | solution.py:172
  817.3 3.7 broadcast_multiply_fusion.1
  823.9 107.9 %all-reduce.15.cloned.1.call-done = f32[1,256,128]{1,2,0:T(8,128)} async-done(((f32[1,256,128]{1,2,0:T(8,128)}), f32[1,256,128]{1,2,0:T(8,128)}) %all-reduce.15.cloned.1.call-update) | async-done | bytes 131088 | tf_op jit(solution)/shard_map/psum | solution.py:98
  935.4 93.5 %all-reduce.17.cloned.1.call-done = f32[2,128,128]{2,1,0:T(8,128)} async-done(((f32[2,128,128]{2,1,0:T(8,128)}), f32[2,128,128]{2,1,0:T(8,128)}) %all-reduce.17.cloned.1.call-update) | async-done | bytes 131088 | tf_op jit(solution)/shard_map/psum | solution.py:109
  1029.0 40.9 %all-gather.14.cloned.1.call-done = f32[2,2048,128]{2,1,0:T(8,128)} async-done(((f32[2,128,128]{2,1,0:T(8,128)}), f32[2,2048,128]{2,1,0:T(8,128)}) %all-gather.14.cloned.1.call-update) | async-done | bytes 2097168 | tf_op jit(solution)/shard_map/all_gather | solution.py:172
  1069.9 7.5 fusion.5
  1077.4 3.6 copy.56
  1084.8 3.6 copy.48
  1088.4 3.0 fusion.27
  1092.9 108.2 %all-reduce.19.cloned.1.call-done = f32[1,512,128]{1,2,0:T(8,128)} async-done(((f32[1,512,128]{1,2,0:T(8,128)}), f32[1,512,128]{1,2,0:T(8,128)}) %all-reduce.19.cloned.1.call-update) | async-done | bytes 262160 | tf_op jit(solution)/shard_map/psum | solution.py:98
  1203.4 96.5 %all-reduce.21.cloned.1.call-done = f32[4,128,128]{2,1,0:T(8,128)} async-done(((f32[4,128,128]{2,1,0:T(8,128)}), f32[4,128,128]{2,1,0:T(8,128)}) %all-reduce.21.cloned.1.call-update) | async-done | bytes 262160 | tf_op jit(solution)/shard_map/psum | solution.py:109
  1300.2 6.6 fusion.3
  1308.6 34.7 %all-gather.16.cloned.1.call-done = f32[4,2048,128]{2,1,0:T(8,128)} async-done(((f32[4,128,128]{2,1,0:T(8,128)}), f32[4,2048,128]{2,1,0:T(8,128)}) %all-gather.16.cloned.1.call-update) | async-done | bytes 4194320 | tf_op jit(solution)/shard_map/all_gather | solution.py:172
  1343.3 9.6 fusion
  1352.9 3.8 copy.59
  1361.3 5.5 copy.51
  1366.8 3.7 fusion.30
  1372.0 108.6 %all-reduce.23.cloned.1.call-done = f32[1,512,128]{1,2,0:T(8,128)} async-done(((f32[1,512,128]{1,2,0:T(8,128)}), f32[1,512,128]{1,2,0:T(8,128)}) %all-reduce.23.cloned.1.call-update) | async-done | bytes 262160 | tf_op jit(solution)/shard_map/psum | solution.py:98
  1483.6 95.9 %all-reduce.25.cloned.1.call-done = f32[8,64,128]{2,1,0:T(8,128)} async-done(((f32[8,64,128]{2,1,0:T(8,128)}), f32[8,64,128]{2,1,0:T(8,128)}) %all-reduce.25.cloned.1.call-update) | async-done | bytes 262160 | tf_op jit(solution)/shard_map/psum | solution.py:109
  (144 shorter events, 70.4 us)
Async XLA Ops:
  7.2 270.6 %copy-start = (f32[512,256]{1,0:T(8,128)S(1)}, f32[512,256]{1,0:T(8,128)}, u32[]{:S(2)}) copy-start(f32[512,256]{1,0:T(8,128)} %param.23) | copy-start | bytes 1572868
  7.2 48.1 %all-gather.18.cloned.1.call-start = ((), (), s32[]{:S(2)}) async-start(), calls=%async_computation.15 | async-start | bytes 4456448 | tf_op jit(solution)/shard_map/all_gather | solution.py:14
  9.4 121.8 %reduce-scatter.4.cloned.1.call-start = ((), (), s32[]{:S(2)}) async-start(), calls=%async_computation.3 | async-start | bytes 4456448 | tf_op jit(solution)/shard_map/reduce_scatter | solution.py:71
  69.0 158.4 %copy-start.7 = (f32[128,512]{1,0:T(8,128)S(1)}, f32[128,512]{1,0:T(8,128)}, u32[]{:S(2)}) copy-start(f32[128,512]{1,0:T(8,128)} %param.20) | copy-start | bytes 786436
  69.0 160.7 %copy-start.17 = (s32[4,2]{0,1:T(2,128)S(1)}, s32[4,2]{0,1:T(2,128)}, u32[]{:S(2)}) copy-start(s32[4,2]{0,1:T(2,128)} %param.26) | copy-start | bytes 100
  69.0 158.4 %all-reduce.11.cloned.1.call-start = ((), (), s32[]{:S(2)}) async-start(), calls=%async_computation.4 | async-start | bytes 524288 | tf_op jit(solution)/shard_map/psum | solution.py:72
  131.2 140.2 %all-gather.20.cloned.1.call-start = ((), (), s32[]{:S(2)}) async-start(), calls=%async_computation.16 | async-start | bytes 4456448 | tf_op jit(solution)/shard_map/all_gather | solution.py:14
  229.4 112.6 %reduce-scatter.6.cloned.1.call-start = ((), (), s32[]{:S(2)}) async-start(), calls=%async_computation.21 | async-start | bytes 2228224 | tf_op jit(solution)/shard_map/reduce_scatter | solution.py:71
  283.2 153.1 %copy-start.9 = (f32[128,256]{1,0:T(8,128)S(1)}, f32[128,256]{1,0:T(8,128)}, u32[]{:S(2)}) copy-start(f32[128,256]{1,0:T(8,128)} %param.19) | copy-start | bytes 393220
  283.2 153.1 %copy-start.16 = (f32[2,128,128]{2,1,0:T(8,128)S(1)}, f32[2,128,128]{2,1,0:T(8,128)}, u32[]{:S(2)}) copy-start(f32[2,128,128]{2,1,0:T(8,128)} %param.15) | copy-start | bytes 393220
  283.2 155.0 %copy-start.18 = (s32[2,1]{0,1:T(1,128)S(1)}, s32[2,1]{0,1:T(1,128)}, u32[]{:S(2)}) copy-start(s32[2,1]{0,1:T(1,128)} %param.25) | copy-start | bytes 28
  283.3 153.1 %all-reduce.27.cloned.1.call-start = ((), (), s32[]{:S(2)}) async-start(), calls=%async_computation.19 | async-start | bytes 262144 | tf_op jit(solution)/shard_map/psum | solution.py:72
  342.0 136.1 %all-gather.22.cloned.1.call-start = ((), (), s32[]{:S(2)}) async-start(), calls=%async_computation.17 | async-start | bytes 2228224 | tf_op jit(solution)/shard_map/all_gather | solution.py:14
  438.2 106.7 %reduce-scatter.8.cloned.1.call-start = ((), (), s32[]{:S(2)}) async-start(), calls=%async_computation.22 | async-start | bytes 2228224 | tf_op jit(solution)/shard_map/reduce_scatter | solution.py:71
  486.4 153.3 %copy-start.6 = (f32[256,256]{1,0:T(8,128)S(1)}, f32[256,256]{1,0:T(8,128)}, u32[]{:S(2)}) copy-start(f32[256,256]{1,0:T(8,128)} %param.18) | copy-start | bytes 786436
  486.4 153.3 %copy-start.15 = (f32[1,256,128]{2,1,0:T(8,128)S(1)}, f32[1,256,128]{2,1,0:T(8,128)}, u32[]{:S(2)}) copy-start(f32[1,256,128]{2,1,0:T(8,128)} %param.14) | copy-start | bytes 393220
  486.4 153.3 %all-reduce.29.cloned.1.call-start = ((), (), s32[]{:S(2)}) async-start(), calls=%async_computation.20 | async-start | bytes 262144 | tf_op jit(solution)/shard_map/psum | solution.py:72
  544.9 136.3 %all-gather.24.cloned.1.call-start = ((), (), s32[]{:S(2)}) async-start(), calls=%async_computation.18 | async-start | bytes 2228224 | tf_op jit(solution)/shard_map/all_gather | solution.py:14
  641.7 134.6 %all-reduce.13.cloned.1.call-start = ((), (), s32[]{:S(2)}) async-start(), calls=%async_computation.5 | async-start | bytes 262144 | tf_op jit(solution)/shard_map/psum | solution.py:109
  684.9 132.3 %all-gather.12.cloned.1.call-start = ((), (), s32[]{:S(2)}) async-start(), calls=%async_computation.6 | async-start | bytes 2228224 | tf_op jit(solution)/shard_map/all_gather | solution.py:172
  776.3 155.4 %all-reduce.15.cloned.1.call-start = ((), (), s32[]{:S(2)}) async-start(), calls=%async_computation.7 | async-start | bytes 262144 | tf_op jit(solution)/shard_map/psum | solution.py:98
  823.8 205.1 %all-reduce.17.cloned.1.call-start = ((), (), s32[]{:S(2)}) async-start(), calls=%async_computation.8 | async-start | bytes 262144 | tf_op jit(solution)/shard_map/psum | solution.py:109
  935.3 134.6 %all-gather.14.cloned.1.call-start = ((), (), s32[]{:S(2)}) async-start(), calls=%async_computation.9 | async-start | bytes 2228224 | tf_op jit(solution)/shard_map/all_gather | solution.py:172
  1028.9 172.2 %all-reduce.19.cloned.1.call-start = ((), (), s32[]{:S(2)}) async-start(), calls=%async_computation.10 | async-start | bytes 524288 | tf_op jit(solution)/shard_map/psum | solution.py:98
  1092.9 207.1 %all-reduce.21.cloned.1.call-start = ((), (), s32[]{:S(2)}) async-start(), calls=%async_computation.11 | async-start | bytes 524288 | tf_op jit(solution)/shard_map/psum | solution.py:109
  1203.3 140.0 %all-gather.16.cloned.1.call-start = ((), (), s32[]{:S(2)}) async-start(), calls=%async_computation.12 | async-start | bytes 4456448 | tf_op jit(solution)/shard_map/all_gather | solution.py:172
  1299.9 180.7 %all-reduce.23.cloned.1.call-start = ((), (), s32[]{:S(2)}) async-start(), calls=%async_computation.13 | async-start | bytes 524288 | tf_op jit(solution)/shard_map/psum | solution.py:98
  1366.8 113.9 %copy-start.14 = (f32[64,512]{1,0:T(8,128)S(1)}, f32[64,512]{1,0:T(8,128)}, u32[]{:S(2)}) copy-start(f32[64,512]{1,0:T(8,128)} %param.21) | copy-start | bytes 393220
  1370.5 112.3 %copy-start.12 = (f32[1,256,128]{1,2,0:T(8,128)S(1)}, f32[1,256,128]{1,2,0:T(8,128)}, u32[]{:S(2)}) copy-start(f32[1,256,128]{1,2,0:T(8,128)} %all-reduce.13.cloned.1.call-done) | copy-start | bytes 393220
  1370.5 209.0 %copy-start.13 = (f32[2,128,128]{2,1,0:T(8,128)S(1)}, f32[2,128,128]{2,1,0:T(8,128)}, u32[]{:S(2)}) copy-start(f32[2,128,128]{2,1,0:T(8,128)} %all-reduce.17.cloned.1.call-done) | copy-start | bytes 393220
  1370.5 209.6 %copy-start.8 = (f32[4,128,128]{2,1,0:T(8,128)S(1)}, f32[4,128,128]{2,1,0:T(8,128)}, u32[]{:S(2)}) copy-start(f32[4,128,128]{2,1,0:T(8,128)} %all-reduce.21.cloned.1.call-done) | copy-start | bytes 786436
  1372.0 207.5 %all-reduce.25.cloned.1.call-start = ((), (), s32[]{:S(2)}) async-start(), calls=%async_computation.14 | async-start | bytes 524288 | tf_op jit(solution)/shard_map/psum | solution.py:109
  (7 other events, 14.6 us)
Sparse Core Ops, SparseCore 0:
  10.4 44.8 all-gather.17
  69.1 61.9 reduce-scatter.3
  134.3 93.0 all-reduce.10
  229.6 41.6 all-gather.19
  283.4 58.5 reduce-scatter.5
  345.0 91.3 all-reduce.26
  438.8 39.2 all-gather.21
  486.5 58.3 reduce-scatter.7
  548.1 91.5 all-reduce.28
  642.0 39.2 all-gather.23
  685.1 91.1 all-reduce.12
  778.0 39.2 all-gather.11
  823.9 107.7 all-reduce.14
  935.4 93.4 all-reduce.16
  1030.6 39.2 all-gather.13
  1093.0 108.0 all-reduce.18
  1204.7 95.1 all-reduce.20
  1301.6 41.6 all-gather.15
  1372.1 108.4 all-reduce.22
  1484.2 95.1 all-reduce.24
